TPU v7x, 32 devices: a whole 2x2x4 slice. The times are simulated.
32 devices in a mesh: grp: 2 (over core), dp: 16 (over z, y, x).
Axes of the slice: x: 2, y: 2, z: 4, core: 2. Of those that a mesh axis runs over, the one named last changes fastest.
Arguments:
- hidden: bfloat16 [32768, 768], P(('grp', 'dp')), may hold values from -6 to 6
- grad_out: bfloat16 [32768, 768], P(('grp', 'dp')), may hold values from -6 to 6
- seq_lens: int32 [64], P(('grp', 'dp')), may hold values from 128 to 512, as said below
- mix_state: float32 [4, 5, 768, 384], P(None, None, ('grp', 'dp')), as said below
- out_state: float32 [4, 768, 768], P(None, ('grp', 'dp')), as said below
- depth_state: float32 [4, 9, 768], replicated, as said below
- span_state: float32 [4, 384, 54], replicated, as said below
- norm_state: float32 [4, 4, 768], replicated, as said below
- up_state: float32 [4, 2, 384, 1536], P(None, 'grp', None, 'dp'), as said below
- bias_state: float32 [4, 2, 1536], P(None, 'grp', 'dp'), as said below
- down_state: float32 [4, 2, 1536, 384], P(None, 'grp', 'dp'), as said below
Outputs:
- out: bfloat16 [32768, 768], P(('grp', 'dp'))
- input_grad: bfloat16 [32768, 768], P(('grp', 'dp'))
- mix_new: float32 [2, 5, 768, 384], P(None, None, ('grp', 'dp'))
- mix_moments: float32 [2, 5, 768, 384], P(None, None, ('grp', 'dp'))
- out_new: float32 [2, 768, 768], P(None, ('grp', 'dp'))
- out_moments: float32 [2, 768, 768], P(None, ('grp', 'dp'))
- depth_new: float32 [2, 9, 768], replicated
- depth_moments: float32 [2, 9, 768], replicated
- span_new: float32 [2, 384, 54], replicated
- span_moments: float32 [2, 384, 54], replicated
- norm_new: float32 [2, 4, 768], replicated
- norm_moments: float32 [2, 4, 768], replicated
- up_new: float32 [2, 2, 384, 1536], P(None, 'grp', None, 'dp')
- up_moments: float32 [2, 2, 384, 1536], P(None, 'grp', None, 'dp')
- bias_new: float32 [2, 2, 1536], P(None, 'grp', 'dp')
- bias_moments: float32 [2, 2, 1536], P(None, 'grp', 'dp')
- down_new: float32 [2, 2, 1536, 384], P(None, 'grp', 'dp')
- down_moments: float32 [2, 2, 1536, 384], P(None, 'grp', 'dp')
Inputs may be any that keep to these rules, and one draw needn't show every extreme that they name: The first seq_lens positions of a sequence are live keys, the rest padding; the first sequence is full. `mix_state`: slot 2 is positive. `out_state`: slot 2 is positive. `depth_state`: slot 2 is positive. `span_state`: slot 2 is positive. `norm_state`: slot 2 is positive. `up_state`: slot 2 is positive. `bias_state`: slot 2 is positive. `down_state`: slot 2 is positive.
All inputs are finite; a program needn't handle non-finite values.
Results may differ from a plain program's by a relative error of at most 0.029.
Values may be sent and summed in bfloat16 or wider, within the bound.
No kernel may reach another device: no remote copies, remote signals or barrier semaphores. Data moves between devices by JAX's collectives and lax.ppermute only.
A program may use at most 192 MiB of HBM per device.

v0:
```python
import jax
import jax.numpy as jnp
from jax import lax
from jax.sharding import PartitionSpec as P

HEADS = 6
HS = 64
KERNEL = 9
STEP = 7
beta_one = 0.9
beta_two = 0.999
adam_eps = 1e-06
ema_rate = 0.99
decay_rate = 0.01
rate_mix = 0.06
rate_out = 0.12
rate_depth = 0.4
rate_span = 0.08
rate_norm = 0.5
rate_up = 0.08
rate_bias = 0.3
rate_down = 0.04


def rounded(value):
    return value.astype(jnp.bfloat16).astype(jnp.float32)


def softmax_rows(scores):
    top_score = jnp.max(scores, axis=-1, keepdims=True)
    powers = jnp.exp(scores - top_score)
    return powers / jnp.sum(powers, axis=-1, keepdims=True)


def gelu_exact(value):
    return 0.5 * value * (1.0 + lax.erf(value * 2.0 ** (-0.5)))


def layer_norm(value, scale_row, shift_row):
    centered = value - jnp.mean(value, axis=-1, keepdims=True)
    variance = jnp.mean(centered * centered, axis=-1, keepdims=True)
    return centered * lax.rsqrt(variance + 1e-12) * scale_row + shift_row


def rear_norm(summed, norms):
    return layer_norm(summed, norms[2], norms[3])


def front_part(inputs, mix, depth, span):
    count, length, width = inputs.shape
    reach = KERNEL // 2
    flat = inputs.reshape(count * length, width)
    queries = rounded(jnp.dot(flat, mix[0]))
    key_rows = rounded(jnp.dot(flat, mix[1]))
    value_rows = rounded(jnp.dot(flat, mix[2]))
    padded = jnp.pad(inputs, ((0, 0), (reach, reach), (0, 0)))
    spread = depth[0] * padded[:, 0:length]
    for offset in range(1, KERNEL):
        spread = spread + depth[offset] * padded[:, offset : offset + length]
    conv_in = rounded(spread.reshape(count * length, width))
    conv_keys = rounded(jnp.dot(conv_in, mix[3]))
    joined = rounded(conv_keys * queries)
    logits = rounded(jnp.dot(joined, span)).reshape(count, length, HEADS, KERNEL)
    kernel_w = softmax_rows(logits)
    conv_vals = rounded(jnp.dot(flat, mix[4])).reshape(count, length, HEADS, HS)
    conv_pad = jnp.pad(conv_vals, ((0, 0), (reach, reach), (0, 0), (0, 0)))
    convolved = kernel_w[..., 0:1] * conv_pad[:, 0:length]
    for offset in range(1, KERNEL):
        convolved = (
            convolved + kernel_w[..., offset : offset + 1] * conv_pad[:, offset : offset + length]
        )
    return (queries, key_rows, value_rows, convolved.reshape(count * length, width // 2))


def back_part(context, convolved, flat, w_out, norms):
    mixed = rounded(jnp.concatenate([context, convolved], axis=1))
    branch = rounded(jnp.dot(mixed, w_out))
    return layer_norm(branch + flat, norms[0], norms[1])


def scores_of(queries, key_rows, seq_len):
    scores = jnp.einsum(
        "qhd,khd->hqk",
        queries.astype(jnp.bfloat16),
        key_rows.astype(jnp.bfloat16),
        preferred_element_type=jnp.float32,
    ) * HS ** (-0.5)
    places = lax.broadcasted_iota(jnp.int32, scores.shape, 2)
    return jnp.where(places < seq_len, scores, -1000000000.0)


def attend_forward(queries, key_rows, value_rows, seq_len):
    scores = scores_of(queries, key_rows, seq_len)
    top_score = jnp.max(scores, axis=-1, keepdims=True)
    powers = jnp.exp(scores - top_score)
    total = jnp.sum(powers, axis=-1, keepdims=True)
    weights = (powers / total).astype(jnp.bfloat16)
    context = jnp.einsum(
        "hqk,khd->qhd", weights, value_rows.astype(jnp.bfloat16), preferred_element_type=jnp.float32
    )
    return (context, top_score + jnp.log(total))


def attend_backward(queries, key_rows, value_rows, seq_len, log_total, d_context):
    query_low = queries.astype(jnp.bfloat16)
    key_low = key_rows.astype(jnp.bfloat16)
    scores = scores_of(queries, key_rows, seq_len)
    probs = jnp.exp(scores - log_total)
    weights = probs.astype(jnp.bfloat16)
    context_low = d_context.astype(jnp.bfloat16)
    d_weights = rounded(
        jnp.einsum(
            "qhd,khd->hqk",
            context_low,
            value_rows.astype(jnp.bfloat16),
            preferred_element_type=jnp.float32,
        )
    )
    d_scores = (probs * (d_weights - jnp.sum(probs * d_weights, axis=-1, keepdims=True))).astype(
        jnp.bfloat16
    )
    d_queries = jnp.einsum(
        "hqk,khd->qhd", d_scores, key_low, preferred_element_type=jnp.float32
    ) * HS ** (-0.5)
    d_keys = jnp.einsum(
        "hqk,qhd->khd", d_scores, query_low, preferred_element_type=jnp.float32
    ) * HS ** (-0.5)
    d_values = jnp.einsum("hqk,qhd->khd", weights, context_low, preferred_element_type=jnp.float32)
    return (d_queries, d_keys, d_values)


def adamw(opt_state, gradient, step_rate, wd_rate):
    moment_one = beta_one * opt_state[1] + (1.0 - beta_one) * gradient
    moment_two = beta_two * opt_state[2] + (1.0 - beta_two) * gradient * gradient
    scaled_one = moment_one / (1.0 - beta_one**STEP)
    scaled_two = moment_two / (1.0 - beta_two**STEP)
    weight = opt_state[0] - step_rate * (
        scaled_one / (jnp.sqrt(scaled_two) + adam_eps) + wd_rate * opt_state[0]
    )
    average = ema_rate * opt_state[3] + (1.0 - ema_rate) * weight
    return (jnp.stack([weight, average]), jnp.stack([moment_one, moment_two]))


def on_device(
    hidden,
    grad_out,
    seq_lens,
    mix_state,
    out_state,
    depth_state,
    span_state,
    norm_state,
    up_state,
    bias_state,
    down_state,
):
    tokens_dev, width = hidden.shape
    count = seq_lens.shape[0]
    length = tokens_dev // count
    half = width // 2
    shaped = (count, length, HEADS, HS)
    inputs = hidden.astype(jnp.float32).reshape(count, length, width)
    flat = inputs.reshape(tokens_dev, width)
    depth_w = rounded(depth_state[0])
    span_w = rounded(span_state[0])
    norm_w = norm_state[0]
    mix_low = mix_state[0].astype(jnp.bfloat16)
    out_low = out_state[0].astype(jnp.bfloat16)

    def mixer_pass(mix_all, out_all):
        front_out, front_back = jax.vjp(
            front_part, inputs, mix_all.astype(jnp.float32), depth_w, span_w
        )
        queries, key_rows, value_rows, convolved = front_out
        context, log_total = jax.vmap(attend_forward)(
            queries.reshape(shaped), key_rows.reshape(shaped), value_rows.reshape(shaped), seq_lens
        )
        normed, rear_back = jax.vjp(
            back_part,
            context.reshape(tokens_dev, half),
            convolved,
            flat,
            out_all.astype(jnp.float32),
            norm_w,
        )
        return (normed, (front_back, rear_back, queries, key_rows, value_rows, log_total))

    mix_all, out_all = (
        lax.all_gather(mix_low, ("grp", "dp"), axis=1, tiled=True),
        lax.all_gather(out_low, ("grp", "dp"), axis=0, tiled=True),
    )
    normed, saved = mixer_pass(mix_all, out_all)
    up_all, bias_all, down_all = (
        lax.all_gather(up_state[0, 0].astype(jnp.bfloat16), "dp", axis=1, tiled=True),
        lax.all_gather(bias_state[0, 0].astype(jnp.bfloat16), "dp", axis=0, tiled=True),
        lax.all_gather(down_state[0, 0].astype(jnp.bfloat16), "dp", axis=0, tiled=True),
    )
    group_in = lax.all_to_all(
        normed.astype(jnp.bfloat16), "grp", split_axis=1, concat_axis=0, tiled=True
    )
    pre_act = jnp.dot(group_in, up_all, preferred_element_type=jnp.float32) + bias_all.astype(
        jnp.float32
    )
    act_low = gelu_exact(pre_act).astype(jnp.bfloat16)
    group_out = jnp.dot(act_low, down_all, preferred_element_type=jnp.float32).astype(jnp.bfloat16)
    back_out = lax.all_to_all(group_out, "grp", split_axis=0, concat_axis=1, tiled=True)
    summed = normed + back_out.astype(jnp.float32)
    result, norm_back = jax.vjp(rear_norm, summed, norm_w)
    d_summed, d_norms_two = norm_back(grad_out.astype(jnp.float32))
    d_group_out = lax.all_to_all(
        d_summed.astype(jnp.bfloat16), "grp", split_axis=1, concat_axis=0, tiled=True
    )
    d_act = lax.dot_general(
        d_group_out, down_all, (((1,), (1,)), ((), ())), preferred_element_type=jnp.float32
    )
    gelu_value, gelu_back = jax.vjp(gelu_exact, pre_act)
    d_pre = gelu_back(d_act)[0].astype(jnp.bfloat16)
    d_down = lax.dot_general(
        act_low, d_group_out, (((0,), (0,)), ((), ())), preferred_element_type=jnp.float32
    )
    d_up = lax.dot_general(
        group_in, d_pre, (((0,), (0,)), ((), ())), preferred_element_type=jnp.float32
    )
    d_bias = jnp.sum(d_pre, axis=0, dtype=jnp.float32)
    d_group_in = lax.dot_general(
        d_pre, up_all, (((1,), (1,)), ((), ())), preferred_element_type=jnp.float32
    ).astype(jnp.bfloat16)
    d_back_in = lax.all_to_all(d_group_in, "grp", split_axis=0, concat_axis=1, tiled=True)
    d_normed = d_summed + d_back_in.astype(jnp.float32)
    mix_again, out_again = (
        lax.all_gather(mix_low, ("grp", "dp"), axis=1, tiled=True),
        lax.all_gather(out_low, ("grp", "dp"), axis=0, tiled=True),
    )
    mixer_saved = mixer_pass(mix_again, out_again)[1]
    front_back, rear_back, queries, key_rows, value_rows, log_total = mixer_saved
    d_context, d_convolved, d_flat, d_out, d_norms = rear_back(d_normed)
    d_queries, d_keys, d_values = jax.vmap(attend_backward)(
        queries.reshape(shaped),
        key_rows.reshape(shaped),
        value_rows.reshape(shaped),
        seq_lens,
        log_total,
        d_context.reshape(shaped),
    )
    d_inputs, d_mix, d_depth, d_span = front_back(
        (
            d_queries.reshape(tokens_dev, half),
            d_keys.reshape(tokens_dev, half),
            d_values.reshape(tokens_dev, half),
            d_convolved,
        )
    )
    d_inputs, d_mix, d_out, d_depth, d_span, d_norms_one = (
        d_inputs.reshape(tokens_dev, width) + d_flat,
        d_mix,
        d_out,
        d_depth,
        d_span,
        d_norms,
    )
    mix_grad, out_grad = (
        lax.psum_scatter(d_mix, ("grp", "dp"), scatter_dimension=1, tiled=True),
        lax.psum_scatter(d_out, ("grp", "dp"), scatter_dimension=0, tiled=True),
    )
    up_grad, bias_grad, down_grad = (
        lax.psum_scatter(d_up, "dp", scatter_dimension=1, tiled=True),
        lax.psum_scatter(d_bias, "dp", scatter_dimension=0, tiled=True),
        lax.psum_scatter(d_down, "dp", scatter_dimension=0, tiled=True),
    )
    depth_grad, span_grad, norm_grad = lax.psum(
        (d_depth, d_span, d_norms_one + d_norms_two), ("grp", "dp")
    )
    mix_update = adamw(mix_state, mix_grad, rate_mix, decay_rate)
    out_update = adamw(out_state, out_grad, rate_out, decay_rate)
    depth_update = adamw(depth_state, depth_grad, rate_depth, decay_rate)
    span_update = adamw(span_state, span_grad, rate_span, decay_rate)
    norm_update = adamw(norm_state, norm_grad, rate_norm, 0.0)
    up_update = adamw(up_state, up_grad[None], rate_up, decay_rate)
    bias_update = adamw(bias_state, bias_grad[None], rate_bias, 0.0)
    down_update = adamw(down_state, down_grad[None], rate_down, decay_rate)
    return (
        result.astype(jnp.bfloat16),
        d_inputs.astype(jnp.bfloat16),
        mix_update[0],
        mix_update[1],
        out_update[0],
        out_update[1],
        depth_update[0],
        depth_update[1],
        span_update[0],
        span_update[1],
        norm_update[0],
        norm_update[1],
        up_update[0],
        up_update[1],
        bias_update[0],
        bias_update[1],
        down_update[0],
        down_update[1],
    )


def solution(mesh):
    placed = (
        P(("grp", "dp"), None),
        P(("grp", "dp"), None),
        P(("grp", "dp")),
        P(None, None, ("grp", "dp"), None),
        P(None, ("grp", "dp"), None),
        P(),
        P(),
        P(),
        P(None, "grp", None, "dp"),
        P(None, "grp", "dp"),
        P(None, "grp", "dp", None),
    )
    return jax.shard_map(
        on_device,
        mesh=mesh,
        in_specs=placed,
        out_specs=(
            P(("grp", "dp"), None),
            P(("grp", "dp"), None),
            P(None, None, ("grp", "dp"), None),
            P(None, None, ("grp", "dp"), None),
            P(None, ("grp", "dp"), None),
            P(None, ("grp", "dp"), None),
            P(),
            P(),
            P(),
            P(),
            P(),
            P(),
            P(None, "grp", None, "dp"),
            P(None, "grp", None, "dp"),
            P(None, "grp", "dp"),
            P(None, "grp", "dp"),
            P(None, "grp", "dp", None),
            P(None, "grp", "dp", None),
        ),
        check_vma=False,
    )
```

profile of v0, /device:TPU:0, one launch (start us, length us, event | category | flops | bytes accessed | tf_op | source)
XLA Modules:
  0.0 987.0 jit_solution(7047482871832338159)
XLA Ops:
  16.7 43.7 %all-reduce.47 = bf16[1536]{0:T(1024)(128)(2,1)S(1)} all-reduce(bf16[1536]{0:T(1024)(128)(2,1)S(1)} %dynamic-update-slice), channel_id=1, replica_groups=mesh['grp'=2,'dp'=16] {'dp'}, use_global_device_ids=true, to_apply=%add.47 | all-reduce | flops 1536 | bytes 6144
  75.1 39.1 %add_convert_fusion.3 = bf16[2,512,768]{1,0,2:T(2,128)(2,1)S(1)} fusion(f32[2,512,768]{1,0,2:T(2,128)} %reshape.438, f32[768]{0:T(1024)S(1)} %get-tuple-element.102, f32[768]{0:T(1024)S(1)} %get-tuple-element.103, f32[768]{0:T(1024)S(1)} %get-tuple-element.104, f32[768]{0:T(1024)S(1)} %get-tuple-element.105, f32[768]{0:T(1024)S(1)} %get-tuple-element.106, ...), kind=kLoop, calls=%fused_computation.58 | loop fusion | flops 14155776 | bytes 4746240 | tf_op jit(solution)/shard_map/jvp()/convert_element_type | solution.py:26
  147.8 18.1 %add_convert_fusion.6 = bf16[2,512,6,64]{1,0,3,2:T(2,128)(2,1)S(1)} fusion(f32[2,512,6,64]{1,0,3,2:T(2,128)} %reshape.464, f32[2,512,6]{1,0,2:T(2,128)S(1)} %get-tuple-element.181, f32[2,512,6]{1,0,2:T(2,128)S(1)} %get-tuple-element.182, f32[2,512,6]{1,0,2:T(2,128)S(1)} %get-tuple-element.183, f32[2,512,6]{1,0,2:T(2,128)S(1)} %get-tuple-element.184, ...), kind=kLoop, calls=%fused_computation.103 | loop fusion | flops 7077888 | bytes 2580480 | tf_op jit(solution)/shard_map/convert.9
  188.5 4.6 all-to-all-start
  195.8 10.4 %multiply_convert_fusion = (bf16[2048,1536]{1,0:T(8,128)(2,1)}, f32[2048,1536]{1,0:T(8,128)}) fusion(f32[1536]{0:T(1024)} %convert_element_type.299, bf16[2048,384]{1,0:T(8,128)(2,1)} %bitcast.21, bf16[384,1536]{0,1:T(8,128)(2,1)} %all-gather.9.cloned.1.call-done), kind=kOutput, calls=%fused_computation.8 | convolution fusion | flops 2434793472 | bytes 21633024 | tf_op jit(solution)/shard_map/dot_general | solution.py:201
  206.2 40.6 %all-gather.11.cloned.1.call-done = bf16[1536,384]{1,0:T(8,128)(2,1)} async-done(((bf16[96,384]{1,0:T(8,128)(2,1)}), bf16[1536,384]{1,0:T(8,128)(2,1)}) %all-gather.11.cloned.1.call-update) | async-done | bytes 1179664 | tf_op jit(solution)/shard_map/all_gather | solution.py:196
  246.7 7.7 convolution_convert_fusion.2
  257.0 6.1 all_to_all.64
  276.1 6.3 all_to_all.65
  282.4 12.4 %convert_reduce_fusion = (f32[1536]{0:T(1024)}, bf16[2048,1536]{1,0:T(8,128)(2,1)S(1)}) fusion(bf16[2048,384]{1,0:T(8,128)(2,1)S(1)} %bitcast.530, bf16[1536,384]{1,0:T(8,128)(2,1)S(1)} %copy-done.97, f32[2048,1536]{1,0:T(8,128)} %get-tuple-element.208, f32[1536]{0:T(1024)S(1)} %copy-done.92), kind=kOutput, calls=%fused_computation.5 | convolution fusion | flops 2466249216 | bytes 21639168 | tf_op jit(solution)/shard_map/dot_general | solution.py:213
  301.8 6.6 all_to_all.66
  320.0 23.8 %multiply_reduce_fusion.21 = (f32[2,512,6]{1,0,2:T(2,128)S(1)}, f32[2,512,6]{1,0,2:T(2,128)S(1)}, f32[2,512,6]{1,0,2:T(2,128)S(1)}, f32[2,512,6]{1,0,2:T(2,128)S...) fusion(f32[2,512,6,64]{1,0,3,2:T(2,128)} %reshape.468, ...), kind=kLoop, calls=%fused_computation.102 | loop fusion | flops 10561536 | bytes 17743872 | tf_op jit(solution)/shard_map/transpose(jvp())/reduce_sum | solution.py:70
  345.9 5.2 fusion.40
  351.4 8.2 fusion.131
  364.1 6.5 fusion
  370.6 6.8 fusion.2
  385.8 6.1 fusion.30
  391.9 7.7 fusion.27
  399.6 4.9 fusion.132
  418.9 6.3 pad_add_fusion.8
  425.3 10.4 %fusion.20 = bf16[2,512,6,64]{1,0,3,2:T(2,128)(2,1)S(1)} fusion(f32[2,512,6,64]{1,0,3,2:T(2,128)S(1)} %copy-done.23, f32[2,512,6,64]{1,0,3,2:T(2,128)S(1)} %copy-done.24, f32[2,512,6,64]{1,0,3,2:T(2,128)S(1)} %copy-done.25, f32[2,512,6,64]{1,0,3,2:T(2,128)S(1)} %copy-done.26, f32[2,512,6,64]{1,0,3,2:T(2,128)S(1)} %copy-done.27, ...), kind=kLoop, calls=%fused_computation.86 | loop fusion | flops 2752512 | bytes 11796480 | tf_op jit(solution)/shard_map/transpose(jvp())/convert_element_type | solution.py:26
  441.8 5.8 copy.162
  447.6 5.7 reshape.455
  462.3 8.6 copy.164
  471.7 60.5 %multiply_reduce_fusion.9 = (f32[768]{0:T(1024)S(1)}, f32[768]{0:T(1024)S(1)}, f32[768]{0:T(1024)S(1)}, f32[768]{0:T(1024)S(1)}, f32[768]{0:T(1024)S(1)}, /*inde...) fusion(f32[2,512,768]{1,0,2:T(2,128)} %reshape.455, ...), kind=kLoop, calls=%fused_computation.49 | loop fusion | flops 19654656 | bytes 34655232 | tf_op jit(solution)/shard_map/transpose(jvp())/reduce_sum | solution.py:59
  532.4 39.5 %all-reduce.49 = (f32[9,768]{1,0:T(8,128)S(1)}, f32[4,768]{1,0:T(4,128)S(1)}) all-reduce(f32[9,768]{1,0:T(8,128)S(1)} %pad_add_fusion.16, f32[4,768]{1,0:T(4,128)S(1)} %add_add_fusion.3), channel_id=1, replica_groups=mesh['grp'=2,'dp'=16] {'grp','dp'}, use_global_device_ids=true, to_apply=%region_36.37 | all-reduce | flops 9984 | bytes 79872 | tf_op jit(solution)/shard_map/psum | solution.py:270
  573.3 14.2 %pad_add_fusion.1 = f32[2,520,768]{1,0,2:T(2,128)S(1)} fusion(f32[2,512,768]{1,0,2:T(2,128)} %get-tuple-element.146, f32[2,512,768]{1,0,2:T(2,128)} %get-tuple-element.147, f32[2,512,768]{1,0,2:T(2,128)} %get-tuple-element.148), kind=kLoop, calls=%fused_computation.25 | loop fusion | flops 1597440 | bytes 12632064 | tf_op jit(solution)/shard_map/transpose(jvp())/add_any | solution.py:59
  587.6 21.5 %fusion.13 = f32[2,512,768]{1,0,2:T(2,128)S(1)} fusion(f32[2,512,768]{1,0,2:T(2,128)} %copy.162, f32[2,512,768]{1,0,2:T(2,128)S(1)} %copy-done.7, f32[2,512,768]{1,0,2:T(2,128)S(1)} %copy-done.8, f32[2,512,768]{1,0,2:T(2,128)S(1)} %copy-done.9, f32[2,512,768]{1,0,2:T(2,128)S(1)} %copy-done.10, f32[2,512,768]{1,0,2:T(2,128)} %get-tuple-element.144, ...), kind=kLoop, calls=%fused_computation.32 | loop fusion | flops 5505024 | bytes 28311552 | tf_op jit(solution)/shard_map/transpose(jvp())/add_any | solution.py:52
  613.5 41.2 %all-reduce.48 = f32[1536]{0:T(1024)S(1)} all-reduce(f32[1536]{0:T(1024)S(1)} %copy-done.93), channel_id=5, replica_groups=mesh['grp'=2,'dp'=16] {'dp'}, use_global_device_ids=true, to_apply=%region_45.46.clone | all-reduce | flops 1536 | bytes 12288
  660.4 43.6 %reduce-scatter.9.cloned.1.call-done = f32[384,96]{0,1:T(8,128)} async-done(((f32[384,1536]{0,1:T(8,128)}), f32[384,96]{0,1:T(8,128)}) %reduce-scatter.9.cloned.1.call-update) | async-done | bytes 147472 | tf_op jit(solution)/shard_map/reduce_scatter | solution.py:266
  705.9 130.6 %reduce-scatter.11.cloned.1.call-done = f32[96,384]{1,0:T(8,128)} async-done(((f32[1536,384]{1,0:T(8,128)}), f32[96,384]{1,0:T(8,128)}) %reduce-scatter.11.cloned.1.call-update) | async-done | bytes 147472 | tf_op jit(solution)/shard_map/reduce_scatter | solution.py:268
  838.4 139.6 %reduce-scatter.5.cloned.1.call-done = f32[5,24,384]{2,0,1:T(8,128)} async-done(((f32[5,768,384]{2,0,1:T(8,128)}), f32[5,24,384]{2,0,1:T(8,128)}) %reduce-scatter.5.cloned.1.call-update) | async-done | bytes 184336 | tf_op jit(solution)/shard_map/reduce_scatter | solution.py:262
  (374 shorter events, 177.8 us)
Async XLA Ops:
  7.2 62.1 %copy-start.42 = (bf16[1024,768]{1,0:T(8,128)(2,1)S(1)}, bf16[1024,768]{1,0:T(8,128)(2,1)}, u32[]{:S(2)}) copy-start(bf16[1024,768]{1,0:T(8,128)(2,1)} %param.12) | copy-start | bytes 4718596
  7.2 108.7 %all-gather.5.cloned.1.call-start = ((), (), s32[]{:S(2)}) async-start(), calls=%async_computation.8 | async-start | bytes 3041280 | tf_op jit(solution)/shard_map/all_gather | solution.py:189
  9.0 170.4 %all-gather.7.cloned.1.call-start = ((), (), s32[]{:S(2)}) async-start(), calls=%async_computation.9 | async-start | bytes 1216512 | tf_op jit(solution)/shard_map/all_gather | solution.py:190
  10.5 183.3 %all-gather.9.cloned.1.call-start = ((), (), s32[]{:S(2)}) async-start(), calls=%async_computation.10 | async-start | bytes 1253376 | tf_op jit(solution)/shard_map/all_gather | solution.py:194
  12.2 234.6 %all-gather.11.cloned.1.call-start = ((), (), s32[]{:S(2)}) async-start(), calls=%async_computation.11 | async-start | bytes 1253376 | tf_op jit(solution)/shard_map/all_gather | solution.py:196
  118.4 27.4 %copy-start.4 = (bf16[1024,384]{1,0:T(8,128)(2,1)}, bf16[1024,384]{1,0:T(8,128)(2,1)S(1)}, u32[]{:S(2)}) copy-start(bf16[1024,384]{1,0:T(8,128)(2,1)S(1)} %convolution_convert_fusion.9) | copy-start | bytes 2359300
  132.7 38.2 %copy-start.29 = (bf16[2,512,6,64]{1,0,3,2:T(2,128)(2,1)}, bf16[2,512,6,64]{1,0,3,2:T(2,128)(2,1)S(1)}, u32[]{:S(2)}) copy-start(bf16[2,512,6,64]{1,0,3,2:T(2,128)(2,1)S(1)} %convert_element_type.275) | copy-start | bytes 2359300
  147.8 21.3 %copy-start.54 = (f32[2,512,6]{1,0,2:T(2,128)}, f32[2,512,6]{1,0,2:T(2,128)S(1)}, u32[]{:S(2)}) copy-start(f32[2,512,6]{1,0,2:T(2,128)S(1)} %get-tuple-element.186) | copy-start | bytes 73732
  147.8 21.3 %copy-start.55 = (f32[2,512,6]{1,0,2:T(2,128)}, f32[2,512,6]{1,0,2:T(2,128)S(1)}, u32[]{:S(2)}) copy-start(f32[2,512,6]{1,0,2:T(2,128)S(1)} %get-tuple-element.187) | copy-start | bytes 73732
  188.5 7.2 all-to-all-start
  193.1 462.9 %all-reduce.52.cloned.1.call-start = ((), (), s32[]{:S(2)}) async-start(), calls=%async_computation.14 | async-start | bytes 172032 | tf_op jit(solution)/shard_map/psum | solution.py:270
  320.0 23.8 %copy-start.64 = (f32[2,512,6]{1,0,2:T(2,128)S(1)}, f32[2,512,6]{1,0,2:T(2,128)}, u32[]{:S(2)}) copy-start(f32[2,512,6]{1,0,2:T(2,128)} %multiply_divide_fusion) | copy-start | bytes 73732
  320.0 24.9 %copy-start.5 = (bf16[1024,384]{1,0:T(8,128)(2,1)S(1)}, bf16[1024,384]{1,0:T(8,128)(2,1)}, u32[]{:S(2)}) copy-start(bf16[1024,384]{1,0:T(8,128)(2,1)} %copy-done.4) | copy-start | bytes 2359300
  320.0 24.9 %copy-start.14 = (bf16[1024,384]{1,0:T(8,128)(2,1)S(1)}, bf16[1024,384]{1,0:T(8,128)(2,1)}, u32[]{:S(2)}) copy-start(bf16[1024,384]{1,0:T(8,128)(2,1)} %copy-done.13) | copy-start | bytes 2359300
  345.9 312.7 %reduce-scatter.7.cloned.1.call-start = ((), (), s32[]{:S(2)}) async-start(), calls=%async_computation.13 | async-start | bytes 2433024 | tf_op jit(solution)/shard_map/reduce_scatter | solution.py:263
  351.1 352.8 %reduce-scatter.9.cloned.1.call-start = ((), (), s32[]{:S(2)}) async-start(), calls=%async_computation.15 | async-start | bytes 2506752 | tf_op jit(solution)/shard_map/reduce_scatter | solution.py:266
  359.7 476.8 %reduce-scatter.11.cloned.1.call-start = ((), (), s32[]{:S(2)}) async-start(), calls=%async_computation.16 | async-start | bytes 2506752 | tf_op jit(solution)/shard_map/reduce_scatter | solution.py:268
  404.5 573.5 %reduce-scatter.5.cloned.1.call-start = ((), (), s32[]{:S(2)}) async-start(), calls=%async_computation.12 | async-start | bytes 9732096 | tf_op jit(solution)/shard_map/reduce_scatter | solution.py:262
  414.6 22.3 %copy-start.36 = (bf16[48,8,2,512]{3,1,2,0:T(8,128)(2,1)}, bf16[48,8,2,512]{3,1,2,0:T(8,128)(2,1)S(1)}, u32[]{:S(2)}) copy-start(bf16[48,8,2,512]{3,1,2,0:T(8,128)(2,1)S(1)} %copy.200) | copy-start | bytes 2359300
  471.7 100.2 %copy-start.53 = (f32[1,9,768]{2,0,1:T(1,128)S(1)}, f32[1,9,768]{2,0,1:T(1,128)}, u32[]{:S(2)}) copy-start(f32[1,9,768]{2,0,1:T(1,128)} %copy-done.52) | copy-start | bytes 82948
  471.7 100.2 %copy-start.61 = (f32[1,9,768]{2,0,1:T(1,128)S(1)}, f32[1,9,768]{2,0,1:T(1,128)}, u32[]{:S(2)}) copy-start(f32[1,9,768]{2,0,1:T(1,128)} %get-tuple-element.191) | copy-start | bytes 82948
  471.7 100.2 %copy-start.62 = (f32[1,9,768]{2,0,1:T(1,128)S(1)}, f32[1,9,768]{2,0,1:T(1,128)}, u32[]{:S(2)}) copy-start(f32[1,9,768]{2,0,1:T(1,128)} %get-tuple-element.192) | copy-start | bytes 82948
  471.7 100.2 %copy-start.63 = (f32[1,9,768]{2,0,1:T(1,128)S(1)}, f32[1,9,768]{2,0,1:T(1,128)}, u32[]{:S(2)}) copy-start(f32[1,9,768]{2,0,1:T(1,128)} %get-tuple-element.194) | copy-start | bytes 82948
  611.8 42.9 %copy-start.94 = (f32[4,1,96]{2,1,0:T(1,128)S(1)}, f32[4,1,96]{2,1,0:T(1,128)}, u32[]{:S(2)}) copy-start(f32[4,1,96]{2,1,0:T(1,128)} %param.20) | copy-start | bytes 4612
  611.9 43.5 %copy-start.65 = (f32[4,4,768]{2,1,0:T(4,128)S(1)}, f32[4,4,768]{2,1,0:T(4,128)}, u32[]{:S(2)}) copy-start(f32[4,4,768]{2,1,0:T(4,128)} %param.18) | copy-start | bytes 147460
  611.9 44.2 %copy-start.49 = (f32[1,384,54]{1,0,2:T(1,128)S(1)}, f32[1,384,54]{1,0,2:T(1,128)}, u32[]{:S(2)}) copy-start(f32[1,384,54]{1,0,2:T(1,128)} %get-tuple-element.176) | copy-start | bytes 248836
  611.9 44.2 %copy-start.50 = (f32[1,384,54]{1,0,2:T(1,128)S(1)}, f32[1,384,54]{1,0,2:T(1,128)}, u32[]{:S(2)}) copy-start(f32[1,384,54]{1,0,2:T(1,128)} %get-tuple-element.177) | copy-start | bytes 248836
  611.9 44.2 %copy-start.51 = (f32[1,384,54]{1,0,2:T(1,128)S(1)}, f32[1,384,54]{1,0,2:T(1,128)}, u32[]{:S(2)}) copy-start(f32[1,384,54]{1,0,2:T(1,128)} %get-tuple-element.179) | copy-start | bytes 248836
  611.9 46.7 %copy-start.48 = (f32[4,24,768]{2,1,0:T(8,128)S(1)}, f32[4,24,768]{2,1,0:T(8,128)}, u32[]{:S(2)}) copy-start(f32[4,24,768]{2,1,0:T(8,128)} %param.15) | copy-start | bytes 884740
  611.9 92.0 %copy-start.46 = (f32[4,1,384,96]{2,3,1,0:T(8,128)S(1)}, f32[4,1,384,96]{2,3,1,0:T(8,128)}, u32[]{:S(2)}) copy-start(f32[4,1,384,96]{2,3,1,0:T(8,128)} %param.19) | copy-start | bytes 1769476
  613.5 223.0 %copy-start.47 = (f32[4,1,96,384]{3,2,1,0:T(8,128)S(1)}, f32[4,1,96,384]{3,2,1,0:T(8,128)}, u32[]{:S(2)}) copy-start(f32[4,1,96,384]{3,2,1,0:T(8,128)} %param.21) | copy-start | bytes 1769476
  658.6 319.4 %copy-start.45 = (f32[4,5,24,384]{3,2,1,0:T(8,128)S(1)}, f32[4,5,24,384]{3,2,1,0:T(8,128)}, u32[]{:S(2)}) copy-start(f32[4,5,24,384]{3,2,1,0:T(8,128)} %param.14) | copy-start | bytes 2211844
  (80 other events, 490.6 us)
Sparse Core Ops, SparseCore 0:
  11.5 61.9 all-gather.4
  77.0 52.9 all-gather.6
  133.4 55.0 all-gather.8
  191.7 54.9 all-gather.10
  346.0 118.3 all-reduce.51
  469.5 100.9 reduce-scatter.6
  576.3 127.6 reduce-scatter.8
  708.9 127.5 reduce-scatter.10
  843.4 134.5 reduce-scatter.4
where the time goes:
time: 998 us; the launch traced here: 987 us
  waiting for transfers between devices  356 us (36%)
  other arithmetic  235 us (24%)
  blocking collectives  143 us (14%)
  matrix products  120 us (12%)
  local copies, waits for them, and re-layouts  110 us (11%)
  between operations  17.2 us (2%)
    reduce_scatter x1, waiting for transfers between devices, on_device(): lax.psum_scatter(d_mix, ('grp', 'dp'), scatter_dimension=1, tiled=True)  140 us
    reduce_scatter x1, waiting for transfers between devices, on_device(): lax.psum_scatter(d_down, 'dp', scatter_dimension=0, tiled=True)  131 us
    unnamed x2, blocking collectives  84.9 us
    reduce_sum x1, other arithmetic, front_part(): spread = spread + depth[offset] * padded[:, offset:offset + length]  60.5 us
    convert_element_type x4, other arithmetic, rounded(): return value.astype(jnp.bfloat16).astype(jnp.float32)  49.7 us
    reduce_scatter x1, waiting for transfers between devices, on_device(): lax.psum_scatter(d_up, 'dp', scatter_dimension=1, tiled=True)  43.6 us
    all_gather x1, waiting for transfers between devices, on_device(): lax.all_gather(down_state[0, 0].astype(jnp.bfloat16), 'dp', axis=0, tiled...  40.6 us
    psum x1, blocking collectives, on_device(): lax.psum((d_depth, d_span, d_norms_one + d_norms_two), ('grp', 'dp'))  39.5 us
  transfers between devices with their start and end apart: 10, of which 5 were waited for; matrix products, arithmetic and copies ran while one was open for 38% of the time, Pallas kernels for 0%

commit v1 on v0

--- a/solution.py
+++ b/solution.py
@@ -20,6 +20,21 @@
 rate_up = 0.08
 rate_bias = 0.3
 rate_down = 0.04
+
+
+def make_the_bars(my_data):
+    then, state_now = (lax.axis_size("dp"), lax.axis_index("dp"))
+    before, big = (my_data, 1)
+    while big < then:
+        pages = []
+        for it in range(then):
+            pages.append((it, it ^ big))
+        arr_next = lax.ppermute(before, "dp", perm=pages)
+        w1 = jnp.concatenate([before, arr_next], axis=0)
+        side_arr = jnp.concatenate([arr_next, before], axis=0)
+        before = jnp.where(state_now & big == 0, w1, side_arr)
+        big = 2 * big
+    return before
 
 
 def rounded(value):
@@ -193,7 +208,7 @@
     up_all, bias_all, down_all = (
         lax.all_gather(up_state[0, 0].astype(jnp.bfloat16), "dp", axis=1, tiled=True),
         lax.all_gather(bias_state[0, 0].astype(jnp.bfloat16), "dp", axis=0, tiled=True),
-        lax.all_gather(down_state[0, 0].astype(jnp.bfloat16), "dp", axis=0, tiled=True),
+        make_the_bars(down_state[0, 0].astype(jnp.bfloat16)),
     )
     group_in = lax.all_to_all(
         normed.astype(jnp.bfloat16), "grp", split_axis=1, concat_axis=0, tiled=True

time: 998 us -> 954 us (0.956)
  waiting for transfers between devices: 356 us -> 318 us
    all_gather x1 -> x0, waiting for transfers between devices: 40.6 us -> none  [on_device(): lax.all_gather(down_state[0, 0].astype(jnp.bfloat16), 'dp', axis=0, tiled...]
    unnamed x226 -> x228, local copies, waits for them, and re-layouts: 30.5 us -> 30.9 us
  transfers between devices with their start and end apart: 10 -> 13, of which waited for: 5 -> 5; matrix products, arithmetic and copies ran while one was open for 38% -> 39% of each run, Pallas kernels for 0% -> 0%
where the time goes in v1:
time: 954 us; the launch traced here: 949 us
  waiting for transfers between devices  318 us (33%)
  other arithmetic  232 us (24%)
  blocking collectives  141 us (15%)
  matrix products  120 us (13%)
  local copies, waits for them, and re-layouts  108 us (11%)
  between operations  17.3 us (2%)
  starting transfers between devices  11.6 us (1%)
    reduce_scatter x1, waiting for transfers between devices, on_device(): lax.psum_scatter(d_mix, ('grp', 'dp'), scatter_dimension=1, tiled=True)  140 us
    reduce_scatter x1, waiting for transfers between devices, on_device(): lax.psum_scatter(d_down, 'dp', scatter_dimension=0, tiled=True)  131 us
    unnamed x2, blocking collectives  81.1 us
    reduce_sum x1, other arithmetic, front_part(): spread = spread + depth[offset] * padded[:, offset:offset + length]  60.4 us
    convert_element_type x4, other arithmetic, rounded(): return value.astype(jnp.bfloat16).astype(jnp.float32)  49.9 us
    reduce_scatter x1, waiting for transfers between devices, on_device(): lax.psum_scatter(d_up, 'dp', scatter_dimension=1, tiled=True)  42 us
    psum x1, blocking collectives, on_device(): lax.psum((d_depth, d_span, d_norms_one + d_norms_two), ('grp', 'dp'))  40.8 us
    unnamed x228, local copies, waits for them, and re-layouts  30.9 us
  transfers between devices with their start and end apart: 13, of which 5 were waited for; matrix products, arithmetic and copies ran while one was open for 39% of the time, Pallas kernels for 0%

profile of v1, /device:TPU:0, one launch (start us, length us, event | category | flops | bytes accessed | tf_op | source)
XLA Modules:
  0.0 948.5 jit_solution(3330183775668601924)
XLA Ops:
  24.6 39.1 %add_convert_fusion.3 = bf16[2,512,768]{1,0,2:T(2,128)(2,1)S(1)} fusion(f32[2,512,768]{1,0,2:T(2,128)} %reshape.438, f32[768]{0:T(1024)S(1)} %get-tuple-element.102, f32[768]{0:T(1024)S(1)} %get-tuple-element.103, f32[768]{0:T(1024)S(1)} %get-tuple-element.104, f32[768]{0:T(1024)S(1)} %get-tuple-element.105, f32[768]{0:T(1024)S(1)} %get-tuple-element.106, ...), kind=kLoop, calls=%fused_computation.58 | loop fusion | flops 14155776 | bytes 4746240 | tf_op jit(solution)/shard_map/jvp()/convert_element_type | solution.py:41
  73.9 40.3 %all-reduce.47 = bf16[1536]{0:T(1024)(128)(2,1)S(1)} all-reduce(bf16[1536]{0:T(1024)(128)(2,1)S(1)} %dynamic-update-slice), channel_id=1, replica_groups=mesh['grp'=2,'dp'=16] {'dp'}, use_global_device_ids=true, to_apply=%add.47 | all-reduce | flops 1536 | bytes 6144
  165.4 13.6 %add_convert_fusion.6 = bf16[2,512,6,64]{1,0,3,2:T(2,128)(2,1)S(1)} fusion(f32[2,512,6,64]{1,0,3,2:T(2,128)S(1)} %copy-done.6, f32[2,512,6]{1,0,2:T(2,128)S(1)} %get-tuple-element.181, f32[2,512,6]{1,0,2:T(2,128)S(1)} %get-tuple-element.182, f32[2,512,6]{1,0,2:T(2,128)S(1)} %get-tuple-element.183, f32[2,512,6]{1,0,2:T(2,128)S(1)} %get-tuple-element.184, ...), kind=kLoop, calls=%fused_computation.103 | loop fusion | flops 7077888 | bytes 2580480 | tf_op jit(solution)/shard_map/convert.9
  191.1 4.6 all-to-all-start
  198.3 8.2 multiply_convert_fusion
  206.5 7.9 convolution_convert_fusion.2
  217.1 6.3 all_to_all.64
  236.3 6.3 all_to_all.65
  242.6 13.7 %convert_reduce_fusion = (f32[1536]{0:T(1024)}, bf16[2048,1536]{1,0:T(8,128)(2,1)S(1)}) fusion(bf16[2048,384]{1,0:T(8,128)(2,1)S(1)} %bitcast.528, bf16[768,384]{1,0:T(8,128)(2,1)} %collective-permute-done.3, bf16[768,384]{1,0:T(8,128)(2,1)} %maximum_select_fusion.1, pred[]{:T(512)S(6)} %eq.18, f32[2048,1536]{1,0:T(8,128)} %get-tuple-element.208, ...), kind=kOutput, calls=%fused_computation.5 | convolution fusion | flops 2471557632 | bytes 21639168 | tf_op jit(solution)/shard_map/dot_general | solution.py:228
  256.3 4.5 convolution_convert_fusion.1
  263.4 6.6 all_to_all.66
  281.6 23.8 %multiply_reduce_fusion.21 = (f32[2,512,6]{1,0,2:T(2,128)S(1)}, f32[2,512,6]{1,0,2:T(2,128)S(1)}, f32[2,512,6]{1,0,2:T(2,128)S(1)}, f32[2,512,6]{1,0,2:T(2,128)S...) fusion(f32[2,512,6,64]{1,0,3,2:T(2,128)} %reshape.468, ...), kind=kLoop, calls=%fused_computation.102 | loop fusion | flops 10561536 | bytes 17743872 | tf_op jit(solution)/shard_map/transpose(jvp())/reduce_sum | solution.py:85
  307.6 5.2 fusion.40
  313.3 8.2 fusion.133
  326.0 6.5 fusion
  332.5 6.6 fusion.2
  347.5 6.1 fusion.30
  353.6 7.7 fusion.27
  361.3 4.9 fusion.134
  380.6 6.3 pad_add_fusion.8
  387.0 10.6 %fusion.20 = bf16[2,512,6,64]{1,0,3,2:T(2,128)(2,1)S(1)} fusion(f32[2,512,6,64]{1,0,3,2:T(2,128)S(1)} %copy-done.24, f32[2,512,6,64]{1,0,3,2:T(2,128)S(1)} %copy-done.25, f32[2,512,6,64]{1,0,3,2:T(2,128)S(1)} %copy-done.26, f32[2,512,6,64]{1,0,3,2:T(2,128)S(1)} %copy-done.27, f32[2,512,6,64]{1,0,3,2:T(2,128)S(1)} %copy-done.28, ...), kind=kLoop, calls=%fused_computation.86 | loop fusion | flops 2752512 | bytes 11796480 | tf_op jit(solution)/shard_map/transpose(jvp())/convert_element_type | solution.py:41
  403.7 5.8 copy.162
  409.4 5.7 reshape.455
  424.2 8.6 copy.164
  433.6 60.4 %multiply_reduce_fusion.9 = (f32[768]{0:T(1024)S(1)}, f32[768]{0:T(1024)S(1)}, f32[768]{0:T(1024)S(1)}, f32[768]{0:T(1024)S(1)}, f32[768]{0:T(1024)S(1)}, /*inde...) fusion(f32[2,512,768]{1,0,2:T(2,128)} %reshape.455, ...), kind=kLoop, calls=%fused_computation.49 | loop fusion | flops 19654656 | bytes 34655232 | tf_op jit(solution)/shard_map/transpose(jvp())/reduce_sum | solution.py:74
  494.2 40.8 %all-reduce.49 = (f32[9,768]{1,0:T(8,128)S(1)}, f32[4,768]{1,0:T(4,128)S(1)}) all-reduce(f32[9,768]{1,0:T(8,128)S(1)} %pad_add_fusion.16, f32[4,768]{1,0:T(4,128)S(1)} %add_add_fusion.3), channel_id=1, replica_groups=mesh['grp'=2,'dp'=16] {'grp','dp'}, use_global_device_ids=true, to_apply=%region_36.37 | all-reduce | flops 9984 | bytes 79872 | tf_op jit(solution)/shard_map/psum | solution.py:285
  536.5 14.2 %pad_add_fusion.1 = f32[2,520,768]{1,0,2:T(2,128)S(1)} fusion(f32[2,512,768]{1,0,2:T(2,128)} %get-tuple-element.146, f32[2,512,768]{1,0,2:T(2,128)} %get-tuple-element.147, f32[2,512,768]{1,0,2:T(2,128)} %get-tuple-element.148), kind=kLoop, calls=%fused_computation.25 | loop fusion | flops 1597440 | bytes 12632064 | tf_op jit(solution)/shard_map/transpose(jvp())/add_any | solution.py:74
  550.8 21.5 %fusion.13 = f32[2,512,768]{1,0,2:T(2,128)S(1)} fusion(f32[2,512,768]{1,0,2:T(2,128)} %copy.162, f32[2,512,768]{1,0,2:T(2,128)S(1)} %copy-done.8, f32[2,512,768]{1,0,2:T(2,128)S(1)} %copy-done.9, f32[2,512,768]{1,0,2:T(2,128)S(1)} %copy-done.10, f32[2,512,768]{1,0,2:T(2,128)S(1)} %copy-done.11, f32[2,512,768]{1,0,2:T(2,128)} %get-tuple-element.144, ...), kind=kLoop, calls=%fused_computation.32 | loop fusion | flops 5505024 | bytes 28311552 | tf_op jit(solution)/shard_map/transpose(jvp())/add_any | solution.py:67
  576.7 40.8 %all-reduce.48 = f32[1536]{0:T(1024)S(1)} all-reduce(f32[1536]{0:T(1024)S(1)} %copy-done.93), channel_id=5, replica_groups=mesh['grp'=2,'dp'=16] {'dp'}, use_global_device_ids=true, to_apply=%region_45.46.clone | all-reduce | flops 1536 | bytes 12288
  623.2 42.0 %reduce-scatter.9.cloned.1.call-done = f32[384,96]{0,1:T(8,128)} async-done(((f32[384,1536]{0,1:T(8,128)}), f32[384,96]{0,1:T(8,128)}) %reduce-scatter.9.cloned.1.call-update) | async-done | bytes 147472 | tf_op jit(solution)/shard_map/reduce_scatter | solution.py:281
  667.2 130.6 %reduce-scatter.11.cloned.1.call-done = f32[96,384]{1,0:T(8,128)} async-done(((f32[1536,384]{1,0:T(8,128)}), f32[96,384]{1,0:T(8,128)}) %reduce-scatter.11.cloned.1.call-update) | async-done | bytes 147472 | tf_op jit(solution)/shard_map/reduce_scatter | solution.py:283
  799.7 139.7 %reduce-scatter.5.cloned.1.call-done = f32[5,24,384]{2,0,1:T(8,128)} async-done(((f32[5,768,384]{2,0,1:T(8,128)}), f32[5,24,384]{2,0,1:T(8,128)}) %reduce-scatter.5.cloned.1.call-update) | async-done | bytes 184336 | tf_op jit(solution)/shard_map/reduce_scatter | solution.py:277
  (384 shorter events, 184.1 us)
Async XLA Ops:
  7.2 114.8 %all-gather.4.cloned.1.call-start = ((), (), s32[]{:S(2)}) async-start(), calls=%async_computation.8 | async-start | bytes 3041280 | tf_op jit(solution)/shard_map/all_gather | solution.py:204
  8.8 173.1 %all-gather.6.cloned.1.call-start = ((), (), s32[]{:S(2)}) async-start(), calls=%async_computation.9 | async-start | bytes 1216512 | tf_op jit(solution)/shard_map/all_gather | solution.py:205
  10.4 186.0 %all-gather.8.cloned.1.call-start = ((), (), s32[]{:S(2)}) async-start(), calls=%async_computation.10 | async-start | bytes 1253376 | tf_op jit(solution)/shard_map/all_gather | solution.py:209
  11.4 52.4 %collective-permute-start = (bf16[96,384]{1,0:T(8,128)(2,1)S(1)}, bf16[96,384]{1,0:T(8,128)(2,1)S(1)}, u32[]{:S(2)}, u32[]{:S(2)}) collective-permute-start(bf16[96,384]{1,0:T(8,128)(2,1)S(1)} %bitcast_convert_fusion.1), channel_id=1, source_target_pairs={{0,1},{1,0},{2,3},{3,2},{4,5},{5,4},{6,7},{7,6},{8,9},{9,8},{10,11... | collective-permute-start | bytes 221192 | tf_op jit(solution)/shard_map/ppermute | solution.py:32
  24.5 47.9 %copy-start.94 = (u32[32]{0:T(128)S(1)}, u32[32]{0:T(128)}, u32[]{:S(2)}) copy-start(u32[32]{0:T(128)} %constant.268) | copy-start | bytes 388
  63.8 5.4 collective-permute-start.1
  69.3 50.6 %collective-permute-start.2 = (bf16[384,384]{1,0:T(8,128)(2,1)S(1)}, bf16[384,384]{1,0:T(8,128)(2,1)}, u32[]{:S(2)}, u32[]{:S(2)}) collective-permute-start(bf16[384,384]{1,0:T(8,128)(2,1)S(1)} %maximum_select_fusion.2), channel_id=1, source_target_pairs={{0,4},{1,5},{2,6},{3,7},{4,0},{5,1},{6,2},{7,3},{8,12},{9,13},{10,... | collective-permute-start | bytes 884744 | tf_op jit(solution)/shard_map/ppermute | solution.py:32
  121.9 84.6 %collective-permute-start.3 = (bf16[768,384]{1,0:T(8,128)(2,1)}, bf16[768,384]{1,0:T(8,128)(2,1)}, u32[]{:S(2)}, u32[]{:S(2)}) collective-permute-start(bf16[768,384]{1,0:T(8,128)(2,1)} %maximum_select_fusion.1), channel_id=1, source_target_pairs={{0,8},{1,9},{2,10},{3,11},{4,12},{5,13},{6,14},{7,15},{8,0},{9,1},... | collective-permute-start | bytes 1769480 | tf_op jit(solution)/shard_map/ppermute | solution.py:32
  124.5 27.8 %copy-start.4 = (bf16[1024,384]{1,0:T(8,128)(2,1)}, bf16[1024,384]{1,0:T(8,128)(2,1)S(1)}, u32[]{:S(2)}) copy-start(bf16[1024,384]{1,0:T(8,128)(2,1)S(1)} %convolution_convert_fusion.9) | copy-start | bytes 2359300
  191.1 7.2 all-to-all-start
  195.7 423.2 %all-reduce.52.cloned.1.call-start = ((), (), s32[]{:S(2)}) async-start(), calls=%async_computation.13 | async-start | bytes 172032 | tf_op jit(solution)/shard_map/psum | solution.py:285
  281.6 23.8 %copy-start.63 = (f32[2,512,6]{1,0,2:T(2,128)S(1)}, f32[2,512,6]{1,0,2:T(2,128)}, u32[]{:S(2)}) copy-start(f32[2,512,6]{1,0,2:T(2,128)} %multiply_divide_fusion) | copy-start | bytes 73732
  281.6 24.9 %copy-start.5 = (bf16[1024,384]{1,0:T(8,128)(2,1)S(1)}, bf16[1024,384]{1,0:T(8,128)(2,1)}, u32[]{:S(2)}) copy-start(bf16[1024,384]{1,0:T(8,128)(2,1)} %copy-done.4) | copy-start | bytes 2359300
  281.6 24.9 %copy-start.15 = (bf16[1024,384]{1,0:T(8,128)(2,1)S(1)}, bf16[1024,384]{1,0:T(8,128)(2,1)}, u32[]{:S(2)}) copy-start(bf16[1024,384]{1,0:T(8,128)(2,1)} %copy-done.14) | copy-start | bytes 2359300
  307.5 313.9 %reduce-scatter.7.cloned.1.call-start = ((), (), s32[]{:S(2)}) async-start(), calls=%async_computation.12 | async-start | bytes 2433024 | tf_op jit(solution)/shard_map/reduce_scatter | solution.py:278
  312.8 352.5 %reduce-scatter.9.cloned.1.call-start = ((), (), s32[]{:S(2)}) async-start(), calls=%async_computation.14 | async-start | bytes 2506752 | tf_op jit(solution)/shard_map/reduce_scatter | solution.py:281
  321.5 476.2 %reduce-scatter.11.cloned.1.call-start = ((), (), s32[]{:S(2)}) async-start(), calls=%async_computation.15 | async-start | bytes 2506752 | tf_op jit(solution)/shard_map/reduce_scatter | solution.py:283
  366.2 573.2 %reduce-scatter.5.cloned.1.call-start = ((), (), s32[]{:S(2)}) async-start(), calls=%async_computation.11 | async-start | bytes 9732096 | tf_op jit(solution)/shard_map/reduce_scatter | solution.py:277
  376.2 22.5 %copy-start.36 = (bf16[48,8,2,512]{3,1,2,0:T(8,128)(2,1)}, bf16[48,8,2,512]{3,1,2,0:T(8,128)(2,1)S(1)}, u32[]{:S(2)}) copy-start(bf16[48,8,2,512]{3,1,2,0:T(8,128)(2,1)S(1)} %copy.200) | copy-start | bytes 2359300
  433.6 101.5 %copy-start.52 = (f32[1,9,768]{2,0,1:T(1,128)S(1)}, f32[1,9,768]{2,0,1:T(1,128)}, u32[]{:S(2)}) copy-start(f32[1,9,768]{2,0,1:T(1,128)} %copy-done.51) | copy-start | bytes 82948
  433.6 101.5 %copy-start.60 = (f32[1,9,768]{2,0,1:T(1,128)S(1)}, f32[1,9,768]{2,0,1:T(1,128)}, u32[]{:S(2)}) copy-start(f32[1,9,768]{2,0,1:T(1,128)} %get-tuple-element.191) | copy-start | bytes 82948
  433.6 101.5 %copy-start.61 = (f32[1,9,768]{2,0,1:T(1,128)S(1)}, f32[1,9,768]{2,0,1:T(1,128)}, u32[]{:S(2)}) copy-start(f32[1,9,768]{2,0,1:T(1,128)} %get-tuple-element.192) | copy-start | bytes 82948
  433.6 101.5 %copy-start.62 = (f32[1,9,768]{2,0,1:T(1,128)S(1)}, f32[1,9,768]{2,0,1:T(1,128)}, u32[]{:S(2)}) copy-start(f32[1,9,768]{2,0,1:T(1,128)} %get-tuple-element.194) | copy-start | bytes 82948
  575.0 42.5 %copy-start.95 = (f32[4,1,96]{2,1,0:T(1,128)S(1)}, f32[4,1,96]{2,1,0:T(1,128)}, u32[]{:S(2)}) copy-start(f32[4,1,96]{2,1,0:T(1,128)} %param.20) | copy-start | bytes 4612
  575.1 43.2 %copy-start.64 = (f32[4,4,768]{2,1,0:T(4,128)S(1)}, f32[4,4,768]{2,1,0:T(4,128)}, u32[]{:S(2)}) copy-start(f32[4,4,768]{2,1,0:T(4,128)} %param.18) | copy-start | bytes 147460
  575.1 43.8 %copy-start.48 = (f32[1,384,54]{1,0,2:T(1,128)S(1)}, f32[1,384,54]{1,0,2:T(1,128)}, u32[]{:S(2)}) copy-start(f32[1,384,54]{1,0,2:T(1,128)} %get-tuple-element.176) | copy-start | bytes 248836
  575.1 43.8 %copy-start.49 = (f32[1,384,54]{1,0,2:T(1,128)S(1)}, f32[1,384,54]{1,0,2:T(1,128)}, u32[]{:S(2)}) copy-start(f32[1,384,54]{1,0,2:T(1,128)} %get-tuple-element.177) | copy-start | bytes 248836
  575.1 43.8 %copy-start.50 = (f32[1,384,54]{1,0,2:T(1,128)S(1)}, f32[1,384,54]{1,0,2:T(1,128)}, u32[]{:S(2)}) copy-start(f32[1,384,54]{1,0,2:T(1,128)} %get-tuple-element.179) | copy-start | bytes 248836
  575.1 46.3 %copy-start.46 = (f32[4,24,768]{2,1,0:T(8,128)S(1)}, f32[4,24,768]{2,1,0:T(8,128)}, u32[]{:S(2)}) copy-start(f32[4,24,768]{2,1,0:T(8,128)} %param.15) | copy-start | bytes 884740
  575.1 90.1 %copy-start.44 = (f32[4,1,384,96]{2,3,1,0:T(8,128)S(1)}, f32[4,1,384,96]{2,3,1,0:T(8,128)}, u32[]{:S(2)}) copy-start(f32[4,1,384,96]{2,3,1,0:T(8,128)} %param.19) | copy-start | bytes 1769476
  576.7 221.1 %copy-start.45 = (f32[4,1,96,384]{3,2,1,0:T(8,128)S(1)}, f32[4,1,96,384]{3,2,1,0:T(8,128)}, u32[]{:S(2)}) copy-start(f32[4,1,96,384]{3,2,1,0:T(8,128)} %param.21) | copy-start | bytes 1769476
  621.4 318.0 %copy-start.43 = (f32[4,5,24,384]{3,2,1,0:T(8,128)S(1)}, f32[4,5,24,384]{3,2,1,0:T(8,128)}, u32[]{:S(2)}) copy-start(f32[4,5,24,384]{3,2,1,0:T(8,128)} %param.14) | copy-start | bytes 2211844
  (84 other events, 445.0 us)
Sparse Core Ops, SparseCore 0:
  11.5 61.9 all-gather.3
  76.9 56.4 all-gather.5
  136.8 57.3 all-gather.7
  307.6 118.1 all-reduce.51
  431.0 101.0 reduce-scatter.6
  537.6 127.5 reduce-scatter.8
  670.2 127.5 reduce-scatter.10
  804.7 134.7 reduce-scatter.4
